TPU v7x, 32 devices: a whole 2x2x4 slice. The times are simulated.
32 devices in a mesh: pipe: 2 (over y), ctx: 16 (over z, x, core).
Axes of the slice: x: 2, y: 2, z: 4, core: 2. Of those that a mesh axis runs over, the one named last changes fastest.
Arguments:
- saved_qkv: bfloat16 [2, 3, 2048, 2048], P('pipe', None, 'ctx'), may hold values from -6 to 6
- handed: bfloat16 [2, 2048, 2048], P('pipe', 'ctx'), may hold values from -6 to 6
- long_filter: bfloat16 [2, 128, 128], P('pipe'), may hold values from -0.5 to 0.5
- short_filter: bfloat16 [2, 3, 3, 2048], P('pipe'), may hold values from -3.5 to 3.5
- doc_lengths: int32 [16], replicated, may hold values from 1 to 512, 2048 in all
Outputs:
- grad_pre: bfloat16 [2, 3, 2048, 2048], P('pipe', None, 'ctx')
- filter_grad: float32 [2, 128, 128], P('pipe')
Inputs may be any that keep to these rules, and one draw needn't show every extreme that they name: `doc_lengths`: documents lie end to end and sum to 2048 tokens; the longest has exactly 512 tokens.
All inputs are finite; a program needn't handle non-finite values.
Results may differ from a plain program's by a relative error of at most 0.0058.
Values may be sent and summed in bfloat16 or wider, within the bound.
A program may use at most 64 MiB of HBM per device.

v0:
```python
import math
import jax
import jax.numpy as jnp
from jax import lax
from jax.sharding import PartitionSpec as P


def from_behind(shard, axis, by):
    count = lax.axis_size(axis)
    return lax.ppermute(shard, axis, [(i, (i + by) % count) for i in range(count)])


def shifted_2(block, axis, distance):
    devices = range(lax.axis_size(axis))
    route = [(i - distance, i) for i in devices if i - distance in devices]
    return lax.ppermute(block, axis, route)


def back_conv(grad_rows, grad_pos, filt, out_len, members, unroll):
    tap_count = filt.shape[0]
    channels = grad_rows.shape[1]

    def step(total, base):
        for offset in range(unroll):
            lag = base * unroll + offset
            ahead = lax.dynamic_slice_in_dim(grad_rows, lag, out_len, 0).astype(jnp.float32)
            ahead_pos = lax.dynamic_slice_in_dim(grad_pos, lag, out_len, 0)
            weights = jnp.repeat(filt[lag].astype(jnp.float32), members)
            total = total + jnp.where((lag <= ahead_pos)[:, None], ahead * weights[None, :], 0.0)
        return (total, None)

    bases = jnp.arange(tap_count // unroll, dtype=jnp.int32)
    result, _ = lax.scan(step, jnp.zeros((out_len, channels), jnp.float32), bases)
    return result


def body(saved_qkv, handed, long_filter, short_filter, doc_lengths):
    query_rows = saved_qkv[0, 0]
    key_rows = saved_qkv[0, 1]
    value_rows = saved_qkv[0, 2]
    filt = long_filter[0]
    tap_count, groups = filt.shape
    row_count, channels = query_rows.shape
    members = channels // groups
    short_taps = short_filter.shape[2]
    unroll = math.gcd(tap_count, 16)
    devices = lax.axis_size("ctx")
    device_index = lax.axis_index("ctx")
    starts = jnp.cumsum(doc_lengths) - doc_lengths
    global_rows = device_index * row_count + jnp.arange(row_count + tap_count, dtype=jnp.int32)
    latest = jnp.max(jnp.where(starts[None, :] <= global_rows[:, None], starts[None, :], 0), axis=1)
    position = global_rows - latest
    own_pos = position[:row_count]
    incoming = from_behind(handed[0], "pipe", -1)
    product = (key_rows.astype(jnp.float32) * value_rows.astype(jnp.float32)).astype(jnp.bfloat16)
    tail_rows = shifted_2(product, "ctx", 1)
    extended = jnp.concatenate([tail_rows, product], axis=0)
    conv_grad = (incoming.astype(jnp.float32) * query_rows.astype(jnp.float32)).astype(jnp.bfloat16)
    grad_wide = conv_grad.astype(jnp.float32)

    def forward_step(total, base):
        columns = []
        for offset in range(unroll):
            lag = base * unroll + offset
            shifted = lax.dynamic_slice_in_dim(extended, tap_count - lag, row_count, 0).astype(
                jnp.float32
            )
            weights = jnp.repeat(filt[lag].astype(jnp.float32), members)
            usable = (lag <= own_pos)[:, None]
            total = total + jnp.where(usable, shifted * weights[None, :], 0.0)
            pair = jnp.sum(
                (grad_wide * shifted).reshape(row_count, groups, members), axis=2
            ).astype(jnp.bfloat16)
            pair = lax.optimization_barrier(pair).astype(jnp.float32)
            columns.append(jnp.sum(jnp.where(usable, pair, 0.0), axis=0))
        return (total, jnp.stack(columns))

    bases = jnp.arange(tap_count // unroll, dtype=jnp.int32)
    conv_out, filter_cols = lax.scan(
        forward_step, jnp.zeros((row_count, channels), jnp.float32), bases
    )
    filter_sum = filter_cols.reshape(tap_count, groups)
    head_rows = shifted_2(conv_grad, "ctx", -1)
    joined = jnp.concatenate([conv_grad, head_rows], axis=0)
    own_grad = back_conv(joined, position, filt, row_count, members, unroll)
    query_grad = (incoming.astype(jnp.float32) * conv_out).astype(jnp.bfloat16)
    key_grad = (own_grad * value_rows.astype(jnp.float32)).astype(jnp.bfloat16)
    value_grad = (own_grad * key_rows.astype(jnp.float32)).astype(jnp.bfloat16)
    stacked = jnp.stack([query_grad, key_grad, value_grad])
    rim_rows = shifted_2(stacked[:, : short_taps - 1], "ctx", -1)
    stacked_ext = jnp.concatenate([stacked, rim_rows], axis=1)
    weights_all = short_filter[0]
    total = jnp.zeros((3, row_count, channels), jnp.float32)
    for shift_by in range(short_taps):
        usable = (shift_by <= position[shift_by : shift_by + row_count])[None, :, None]
        weights = weights_all[:, shift_by].astype(jnp.float32)[:, None, :]
        total = total + jnp.where(
            usable,
            weights * stacked_ext[:, shift_by : shift_by + row_count].astype(jnp.float32),
            0.0,
        )
    grad_pre = total.astype(jnp.bfloat16)[None]
    summed = lax.psum(filter_sum, "ctx")
    filter_grad = (summed / math.sqrt(row_count * devices * members))[None]
    return (grad_pre, filter_grad)


def solution(mesh):
    return jax.shard_map(
        body,
        mesh=mesh,
        in_specs=(
            P("pipe", None, "ctx", None),
            P("pipe", "ctx", None),
            P("pipe", None, None),
            P("pipe", None, None, None),
            P(),
        ),
        out_specs=(P("pipe", None, "ctx", None), P("pipe", None, None)),
        check_vma=False,
    )
```

profile of v0, /device:TPU:8, one launch (start us, length us, event | category | flops | bytes accessed | tf_op | source)
XLA Modules:
  0.0 410.6 jit_solution(385893030262521515)
XLA Ops:
  7.2 1.6 collective-permute-start
  8.8 12.4 %collective-permute-done = bf16[128,2048]{1,0:T(8,128)(2,1)S(1)} collective-permute-done((bf16[128,2048]{1,0:T(8,128)(2,1)}, bf16[128,2048]{1,0:T(8,128)(2,1)S(1)}, u32[]{:S(2)}, u32[]{:S(2)}) %collective-permute-start) | collective-permute-done | bytes 524320 | tf_op jit(solution)/shard_map/ppermute | solution.py:10
  21.2 1.4 fusion.112
  22.6 1.9 collective-permute-start.2
  24.5 0.7 copy.16
  25.4 0.7 sub.118
  26.2 5.0 %collective-permute-done.2 = bf16[128,2048]{1,0:T(8,128)(2,1)S(1)} collective-permute-done((bf16[128,2048]{1,0:T(8,128)(2,1)S(1)}, bf16[128,2048]{1,0:T(8,128)(2,1)S(1)}, u32[]{:S(2)}, u32[]{:S(2)}) %collective-permute-start.2) | collective-permute-done | bytes 524320 | tf_op jit(solution)/shard_map/ppermute | solution.py:16
  31.3 81.4 %while.30 = (s32[]{:T(128)}, f32[128,2048]{1,0:T(8,128)S(1)}, s32[8]{0:T(128)S(1)}, s32[256]{0:T(256)S(1)}, bf16[256,2048]{1,0:T(8,128)(2,1)S(1)}, /*index=5*/bf...) while((s32[]{:T(128)}, f32[128,2048]{1,0:T(8,128)S(1)}, ...), condition=%wide.region_37.38_spmd.clone, body=%wide.region_36.37_spmd.clone.sunk | while | flops 17043556 | bytes 11044691 | solution.py:33
  31.3 0.7 dynamic_slice.941
  35.9 5.6 %fusion.128 = f32[128,2048]{1,0:T(8,128)S(1)} fusion(f32[128,2048]{1,0:T(8,128)S(1)} %get-tuple-element.835, f32[2048]{0:T(1024)S(1)} %mul.1435, bf16[256,2048]{1,0:T(8,128)(2,1)S(1)} %get-tuple-element.893, s32[]{:T(128)S(6)} %select_n.1196, f32[2048]{0:T(1024)S(1)} %mul.1436, s32[]{:T(128)S(6)} %select_n.1197, f32[2048]{0:T(1024)S(1)} %mul.1437, ...), kind=kLoop, calls=%fused_computation.176.clone.1 | loop fusion | flops 17039360 | bytes 10618945 | tf_op jit(solution)/shard_map/while/body/eval_jaxpr/add | solution.py:29
  41.5 0.7 dynamic_slice.941
  46.1 5.6 %fusion.128 = f32[128,2048]{1,0:T(8,128)S(1)} fusion(f32[128,2048]{1,0:T(8,128)S(1)} %get-tuple-element.835, f32[2048]{0:T(1024)S(1)} %mul.1435, bf16[256,2048]{1,0:T(8,128)(2,1)S(1)} %get-tuple-element.893, s32[]{:T(128)S(6)} %select_n.1196, f32[2048]{0:T(1024)S(1)} %mul.1436, s32[]{:T(128)S(6)} %select_n.1197, f32[2048]{0:T(1024)S(1)} %mul.1437, ...), kind=kLoop, calls=%fused_computation.176.clone.1 | loop fusion | flops 17039360 | bytes 10618945 | tf_op jit(solution)/shard_map/while/body/eval_jaxpr/add | solution.py:29
  51.7 0.7 dynamic_slice.941
  56.2 5.6 %fusion.128 = f32[128,2048]{1,0:T(8,128)S(1)} fusion(f32[128,2048]{1,0:T(8,128)S(1)} %get-tuple-element.835, f32[2048]{0:T(1024)S(1)} %mul.1435, bf16[256,2048]{1,0:T(8,128)(2,1)S(1)} %get-tuple-element.893, s32[]{:T(128)S(6)} %select_n.1196, f32[2048]{0:T(1024)S(1)} %mul.1436, s32[]{:T(128)S(6)} %select_n.1197, f32[2048]{0:T(1024)S(1)} %mul.1437, ...), kind=kLoop, calls=%fused_computation.176.clone.1 | loop fusion | flops 17039360 | bytes 10618945 | tf_op jit(solution)/shard_map/while/body/eval_jaxpr/add | solution.py:29
  61.9 0.7 dynamic_slice.941
  66.4 5.6 %fusion.128 = f32[128,2048]{1,0:T(8,128)S(1)} fusion(f32[128,2048]{1,0:T(8,128)S(1)} %get-tuple-element.835, f32[2048]{0:T(1024)S(1)} %mul.1435, bf16[256,2048]{1,0:T(8,128)(2,1)S(1)} %get-tuple-element.893, s32[]{:T(128)S(6)} %select_n.1196, f32[2048]{0:T(1024)S(1)} %mul.1436, s32[]{:T(128)S(6)} %select_n.1197, f32[2048]{0:T(1024)S(1)} %mul.1437, ...), kind=kLoop, calls=%fused_computation.176.clone.1 | loop fusion | flops 17039360 | bytes 10618945 | tf_op jit(solution)/shard_map/while/body/eval_jaxpr/add | solution.py:29
  72.0 0.7 dynamic_slice.941
  76.6 5.6 %fusion.128 = f32[128,2048]{1,0:T(8,128)S(1)} fusion(f32[128,2048]{1,0:T(8,128)S(1)} %get-tuple-element.835, f32[2048]{0:T(1024)S(1)} %mul.1435, bf16[256,2048]{1,0:T(8,128)(2,1)S(1)} %get-tuple-element.893, s32[]{:T(128)S(6)} %select_n.1196, f32[2048]{0:T(1024)S(1)} %mul.1436, s32[]{:T(128)S(6)} %select_n.1197, f32[2048]{0:T(1024)S(1)} %mul.1437, ...), kind=kLoop, calls=%fused_computation.176.clone.1 | loop fusion | flops 17039360 | bytes 10618945 | tf_op jit(solution)/shard_map/while/body/eval_jaxpr/add | solution.py:29
  82.2 0.7 dynamic_slice.941
  86.7 5.6 %fusion.128 = f32[128,2048]{1,0:T(8,128)S(1)} fusion(f32[128,2048]{1,0:T(8,128)S(1)} %get-tuple-element.835, f32[2048]{0:T(1024)S(1)} %mul.1435, bf16[256,2048]{1,0:T(8,128)(2,1)S(1)} %get-tuple-element.893, s32[]{:T(128)S(6)} %select_n.1196, f32[2048]{0:T(1024)S(1)} %mul.1436, s32[]{:T(128)S(6)} %select_n.1197, f32[2048]{0:T(1024)S(1)} %mul.1437, ...), kind=kLoop, calls=%fused_computation.176.clone.1 | loop fusion | flops 17039360 | bytes 10618945 | tf_op jit(solution)/shard_map/while/body/eval_jaxpr/add | solution.py:29
  92.4 0.7 dynamic_slice.941
  96.9 5.6 %fusion.128 = f32[128,2048]{1,0:T(8,128)S(1)} fusion(f32[128,2048]{1,0:T(8,128)S(1)} %get-tuple-element.835, f32[2048]{0:T(1024)S(1)} %mul.1435, bf16[256,2048]{1,0:T(8,128)(2,1)S(1)} %get-tuple-element.893, s32[]{:T(128)S(6)} %select_n.1196, f32[2048]{0:T(1024)S(1)} %mul.1436, s32[]{:T(128)S(6)} %select_n.1197, f32[2048]{0:T(1024)S(1)} %mul.1437, ...), kind=kLoop, calls=%fused_computation.176.clone.1 | loop fusion | flops 17039360 | bytes 10618945 | tf_op jit(solution)/shard_map/while/body/eval_jaxpr/add | solution.py:29
  102.5 0.7 dynamic_slice.941
  107.1 5.6 %fusion.128 = f32[128,2048]{1,0:T(8,128)S(1)} fusion(f32[128,2048]{1,0:T(8,128)S(1)} %get-tuple-element.835, f32[2048]{0:T(1024)S(1)} %mul.1435, bf16[256,2048]{1,0:T(8,128)(2,1)S(1)} %get-tuple-element.893, s32[]{:T(128)S(6)} %select_n.1196, f32[2048]{0:T(1024)S(1)} %mul.1436, s32[]{:T(128)S(6)} %select_n.1197, f32[2048]{0:T(1024)S(1)} %mul.1437, ...), kind=kLoop, calls=%fused_computation.176.clone.1 | loop fusion | flops 17039360 | bytes 10618945 | tf_op jit(solution)/shard_map/while/body/eval_jaxpr/add | solution.py:29
  112.7 2.6 fusion.118
  115.3 3.8 collective-permute-start.1
  119.5 7.5 %collective-permute-done.1 = bf16[128,2048]{1,0:T(8,128)(2,1)} collective-permute-done((bf16[128,2048]{1,0:T(8,128)(2,1)S(1)}, bf16[128,2048]{1,0:T(8,128)(2,1)}, u32[]{:S(2)}, u32[]{:S(2)}) %collective-permute-start.1) | collective-permute-done | bytes 524320 | tf_op jit(solution)/shard_map/ppermute | solution.py:16
  127.0 2.2 pad_maximum_fusion.2
  129.1 1.5 copy.17
  130.6 178.6 %while.29 = (s32[]{:T(128)}, f32[128,2048]{0,1:T(8,128)S(1)}, f32[8,16,128]{2,1,0:T(8,128)}, s32[8]{0:T(128)S(1)}, s32[128]{0:T(128)S(1)}, /*index=5*/bf16[256,2...) while((s32[]{:T(128)}, f32[128,2048]{0,1:T(8,128)S(1)}, ...), condition=%wide.region_35.36_spmd.clone, body=%wide.region_2.35_spmd.clone.sunk | while | flops 30148740 | bytes 21566524 | solution.py:79
  130.6 0.6 dynamic_slice.921
  132.0 6.9 %bitcast_reduce_fusion.17 = (bf16[128,128]{0,1:T(8,128)(2,1)S(1)}, bf16[128,128]{0,1:T(8,128)(2,1)S(1)}, bf16[128,128]{0,1:T(8,128)(2,1)S(1)}, bf16[128,128]{0,1...) fusion(f32[128,2048]{0,1:T(8,128)S(1)} %get-tuple-element.1035,, ...), kind=kLoop, calls=%fused_computation.64.clone.1 | loop fusion | flops 12320768 | bytes 9961536 | tf_op jit(solution)/shard_map/while/body/eval_jaxpr/reduce_sum | solution.py:71
  140.0 0.6 constant_dynamic-update-slice_fusion.2
  143.3 9.6 %fusion.126 = f32[128,2048]{0,1:T(8,128)S(1)} fusion(f32[128,2048]{0,1:T(8,128)S(1)} %get-tuple-element.987, f32[2048]{0:T(1024)S(1)} %mul.1386, f32[2048]{0:T(1024)S(1)} %mul.1387, f32[2048]{0:T(1024)S(1)} %mul.1388, f32[2048]{0:T(1024)S(1)} %mul.1389, f32[2048]{0:T(1024)S(1)} %mul.1390, f32[2048]{0:T(1024)S(1)} %mul.1391, f32[2048]{0:T(1024)S(1)} %mul.1392, ...), kind=kLoop, calls=%fused_computation.48.clone.1 | loop fusion | flops 17039360 | bytes 10618945 | tf_op jit(solution)/shard_map/while/body/eval_jaxpr/add | solution.py:70
  154.3 6.9 %bitcast_reduce_fusion.17 = (bf16[128,128]{0,1:T(8,128)(2,1)S(1)}, bf16[128,128]{0,1:T(8,128)(2,1)S(1)}, bf16[128,128]{0,1:T(8,128)(2,1)S(1)}, bf16[128,128]{0,1...) fusion(f32[128,2048]{0,1:T(8,128)S(1)} %get-tuple-element.1035,, ...), kind=kLoop, calls=%fused_computation.64.clone.1 | loop fusion | flops 12320768 | bytes 9961536 | tf_op jit(solution)/shard_map/while/body/eval_jaxpr/reduce_sum | solution.py:71
  162.3 0.6 constant_dynamic-update-slice_fusion.2
  165.7 9.6 %fusion.126 = f32[128,2048]{0,1:T(8,128)S(1)} fusion(f32[128,2048]{0,1:T(8,128)S(1)} %get-tuple-element.987, f32[2048]{0:T(1024)S(1)} %mul.1386, f32[2048]{0:T(1024)S(1)} %mul.1387, f32[2048]{0:T(1024)S(1)} %mul.1388, f32[2048]{0:T(1024)S(1)} %mul.1389, f32[2048]{0:T(1024)S(1)} %mul.1390, f32[2048]{0:T(1024)S(1)} %mul.1391, f32[2048]{0:T(1024)S(1)} %mul.1392, ...), kind=kLoop, calls=%fused_computation.48.clone.1 | loop fusion | flops 17039360 | bytes 10618945 | tf_op jit(solution)/shard_map/while/body/eval_jaxpr/add | solution.py:70
  176.7 6.9 %bitcast_reduce_fusion.17 = (bf16[128,128]{0,1:T(8,128)(2,1)S(1)}, bf16[128,128]{0,1:T(8,128)(2,1)S(1)}, bf16[128,128]{0,1:T(8,128)(2,1)S(1)}, bf16[128,128]{0,1...) fusion(f32[128,2048]{0,1:T(8,128)S(1)} %get-tuple-element.1035,, ...), kind=kLoop, calls=%fused_computation.64.clone.1 | loop fusion | flops 12320768 | bytes 9961536 | tf_op jit(solution)/shard_map/while/body/eval_jaxpr/reduce_sum | solution.py:71
  184.7 0.6 constant_dynamic-update-slice_fusion.2
  188.0 9.6 %fusion.126 = f32[128,2048]{0,1:T(8,128)S(1)} fusion(f32[128,2048]{0,1:T(8,128)S(1)} %get-tuple-element.987, f32[2048]{0:T(1024)S(1)} %mul.1386, f32[2048]{0:T(1024)S(1)} %mul.1387, f32[2048]{0:T(1024)S(1)} %mul.1388, f32[2048]{0:T(1024)S(1)} %mul.1389, f32[2048]{0:T(1024)S(1)} %mul.1390, f32[2048]{0:T(1024)S(1)} %mul.1391, f32[2048]{0:T(1024)S(1)} %mul.1392, ...), kind=kLoop, calls=%fused_computation.48.clone.1 | loop fusion | flops 17039360 | bytes 10618945 | tf_op jit(solution)/shard_map/while/body/eval_jaxpr/add | solution.py:70
  197.6 0.6 dynamic_slice.921
  199.0 6.9 %bitcast_reduce_fusion.17 = (bf16[128,128]{0,1:T(8,128)(2,1)S(1)}, bf16[128,128]{0,1:T(8,128)(2,1)S(1)}, bf16[128,128]{0,1:T(8,128)(2,1)S(1)}, bf16[128,128]{0,1...) fusion(f32[128,2048]{0,1:T(8,128)S(1)} %get-tuple-element.1035,, ...), kind=kLoop, calls=%fused_computation.64.clone.1 | loop fusion | flops 12320768 | bytes 9961536 | tf_op jit(solution)/shard_map/while/body/eval_jaxpr/reduce_sum | solution.py:71
  207.0 0.6 constant_dynamic-update-slice_fusion.2
  210.3 9.6 %fusion.126 = f32[128,2048]{0,1:T(8,128)S(1)} fusion(f32[128,2048]{0,1:T(8,128)S(1)} %get-tuple-element.987, f32[2048]{0:T(1024)S(1)} %mul.1386, f32[2048]{0:T(1024)S(1)} %mul.1387, f32[2048]{0:T(1024)S(1)} %mul.1388, f32[2048]{0:T(1024)S(1)} %mul.1389, f32[2048]{0:T(1024)S(1)} %mul.1390, f32[2048]{0:T(1024)S(1)} %mul.1391, f32[2048]{0:T(1024)S(1)} %mul.1392, ...), kind=kLoop, calls=%fused_computation.48.clone.1 | loop fusion | flops 17039360 | bytes 10618945 | tf_op jit(solution)/shard_map/while/body/eval_jaxpr/add | solution.py:70
  219.9 0.6 dynamic_slice.921
  221.3 6.9 %bitcast_reduce_fusion.17 = (bf16[128,128]{0,1:T(8,128)(2,1)S(1)}, bf16[128,128]{0,1:T(8,128)(2,1)S(1)}, bf16[128,128]{0,1:T(8,128)(2,1)S(1)}, bf16[128,128]{0,1...) fusion(f32[128,2048]{0,1:T(8,128)S(1)} %get-tuple-element.1035,, ...), kind=kLoop, calls=%fused_computation.64.clone.1 | loop fusion | flops 12320768 | bytes 9961536 | tf_op jit(solution)/shard_map/while/body/eval_jaxpr/reduce_sum | solution.py:71
  229.3 0.6 constant_dynamic-update-slice_fusion.2
  232.7 9.6 %fusion.126 = f32[128,2048]{0,1:T(8,128)S(1)} fusion(f32[128,2048]{0,1:T(8,128)S(1)} %get-tuple-element.987, f32[2048]{0:T(1024)S(1)} %mul.1386, f32[2048]{0:T(1024)S(1)} %mul.1387, f32[2048]{0:T(1024)S(1)} %mul.1388, f32[2048]{0:T(1024)S(1)} %mul.1389, f32[2048]{0:T(1024)S(1)} %mul.1390, f32[2048]{0:T(1024)S(1)} %mul.1391, f32[2048]{0:T(1024)S(1)} %mul.1392, ...), kind=kLoop, calls=%fused_computation.48.clone.1 | loop fusion | flops 17039360 | bytes 10618945 | tf_op jit(solution)/shard_map/while/body/eval_jaxpr/add | solution.py:70
  242.3 0.6 dynamic_slice.921
  243.6 6.9 %bitcast_reduce_fusion.17 = (bf16[128,128]{0,1:T(8,128)(2,1)S(1)}, bf16[128,128]{0,1:T(8,128)(2,1)S(1)}, bf16[128,128]{0,1:T(8,128)(2,1)S(1)}, bf16[128,128]{0,1...) fusion(f32[128,2048]{0,1:T(8,128)S(1)} %get-tuple-element.1035,, ...), kind=kLoop, calls=%fused_computation.64.clone.1 | loop fusion | flops 12320768 | bytes 9961536 | tf_op jit(solution)/shard_map/while/body/eval_jaxpr/reduce_sum | solution.py:71
  251.6 0.6 constant_dynamic-update-slice_fusion.2
  255.0 9.6 %fusion.126 = f32[128,2048]{0,1:T(8,128)S(1)} fusion(f32[128,2048]{0,1:T(8,128)S(1)} %get-tuple-element.987, f32[2048]{0:T(1024)S(1)} %mul.1386, f32[2048]{0:T(1024)S(1)} %mul.1387, f32[2048]{0:T(1024)S(1)} %mul.1388, f32[2048]{0:T(1024)S(1)} %mul.1389, f32[2048]{0:T(1024)S(1)} %mul.1390, f32[2048]{0:T(1024)S(1)} %mul.1391, f32[2048]{0:T(1024)S(1)} %mul.1392, ...), kind=kLoop, calls=%fused_computation.48.clone.1 | loop fusion | flops 17039360 | bytes 10618945 | tf_op jit(solution)/shard_map/while/body/eval_jaxpr/add | solution.py:70
  266.0 6.9 %bitcast_reduce_fusion.17 = (bf16[128,128]{0,1:T(8,128)(2,1)S(1)}, bf16[128,128]{0,1:T(8,128)(2,1)S(1)}, bf16[128,128]{0,1:T(8,128)(2,1)S(1)}, bf16[128,128]{0,1...) fusion(f32[128,2048]{0,1:T(8,128)S(1)} %get-tuple-element.1035,, ...), kind=kLoop, calls=%fused_computation.64.clone.1 | loop fusion | flops 12320768 | bytes 9961536 | tf_op jit(solution)/shard_map/while/body/eval_jaxpr/reduce_sum | solution.py:71
  274.0 0.6 constant_dynamic-update-slice_fusion.2
  277.3 9.6 %fusion.126 = f32[128,2048]{0,1:T(8,128)S(1)} fusion(f32[128,2048]{0,1:T(8,128)S(1)} %get-tuple-element.987, f32[2048]{0:T(1024)S(1)} %mul.1386, f32[2048]{0:T(1024)S(1)} %mul.1387, f32[2048]{0:T(1024)S(1)} %mul.1388, f32[2048]{0:T(1024)S(1)} %mul.1389, f32[2048]{0:T(1024)S(1)} %mul.1390, f32[2048]{0:T(1024)S(1)} %mul.1391, f32[2048]{0:T(1024)S(1)} %mul.1392, ...), kind=kLoop, calls=%fused_computation.48.clone.1 | loop fusion | flops 17039360 | bytes 10618945 | tf_op jit(solution)/shard_map/while/body/eval_jaxpr/add | solution.py:70
  288.3 6.9 %bitcast_reduce_fusion.17 = (bf16[128,128]{0,1:T(8,128)(2,1)S(1)}, bf16[128,128]{0,1:T(8,128)(2,1)S(1)}, bf16[128,128]{0,1:T(8,128)(2,1)S(1)}, bf16[128,128]{0,1...) fusion(f32[128,2048]{0,1:T(8,128)S(1)} %get-tuple-element.1035,, ...), kind=kLoop, calls=%fused_computation.64.clone.1 | loop fusion | flops 12320768 | bytes 9961536 | tf_op jit(solution)/shard_map/while/body/eval_jaxpr/reduce_sum | solution.py:71
  296.3 0.6 constant_dynamic-update-slice_fusion.2
  299.6 9.6 %fusion.126 = f32[128,2048]{0,1:T(8,128)S(1)} fusion(f32[128,2048]{0,1:T(8,128)S(1)} %get-tuple-element.987, f32[2048]{0:T(1024)S(1)} %mul.1386, f32[2048]{0:T(1024)S(1)} %mul.1387, f32[2048]{0:T(1024)S(1)} %mul.1388, f32[2048]{0:T(1024)S(1)} %mul.1389, f32[2048]{0:T(1024)S(1)} %mul.1390, f32[2048]{0:T(1024)S(1)} %mul.1391, f32[2048]{0:T(1024)S(1)} %mul.1392, ...), kind=kLoop, calls=%fused_computation.48.clone.1 | loop fusion | flops 17039360 | bytes 10618945 | tf_op jit(solution)/shard_map/while/body/eval_jaxpr/add | solution.py:70
  309.6 1.2 fusion.119
  311.0 1.9 collective-permute-start.3
  313.0 1.4 collective-permute-done.3
  314.6 2.6 fusion.111
  317.2 85.1 %all-reduce.2.cloned.1.call-done = f32[128,128]{1,0:T(8,128)} async-done(((f32[128,128]{1,0:T(8,128)}), f32[128,128]{1,0:T(8,128)}) %all-reduce.2.cloned.1.call-update) | async-done | bytes 65552 | tf_op jit(solution)/shard_map/psum | solution.py:103
  402.2 1.5 multiply_bitcast_fusion
  (665 shorter events, 57.6 us)
Async XLA Ops:
  7.2 395.1 %all-reduce.2.cloned.1.call-start = ((), (), s32[]{:S(2)}) async-start(), calls=%async_computation | async-start | bytes 131072 | tf_op jit(solution)/shard_map/psum | solution.py:103
  7.2 24.1 %copy-start.5 = (bf16[1,128,128]{2,1,0:T(8,128)(2,1)S(1)}, bf16[1,128,128]{2,1,0:T(8,128)(2,1)}, u32[]{:S(2)}) copy-start(bf16[1,128,128]{2,1,0:T(8,128)(2,1)} %param.11) | copy-start | bytes 98308
  7.2 13.9 %collective-permute-start = (bf16[128,2048]{1,0:T(8,128)(2,1)}, bf16[128,2048]{1,0:T(8,128)(2,1)S(1)}, u32[]{:S(2)}, u32[]{:S(2)}) collective-permute-start(bf16[128,2048]{1,0:T(8,128)(2,1)} %bitcast.309), channel_id=1, source_target_pairs={{0,16},{16,0},{1,17},{17,1},{2,18},{18,2},{3,19},{19,3},{4,20},{20... | collective-permute-start | bytes 1572872 | tf_op jit(solution)/shard_map/ppermute | solution.py:10
  21.2 3.4 copy-start.4
  22.6 8.7 %copy-start.2 = (bf16[128,2048]{1,0:T(8,128)(2,1)}, bf16[128,2048]{1,0:T(8,128)(2,1)S(1)}, u32[]{:S(2)}) copy-start(bf16[128,2048]{1,0:T(8,128)(2,1)S(1)} %fusion.112) | copy-start | bytes 1572868
  22.6 8.6 %collective-permute-start.2 = (bf16[128,2048]{1,0:T(8,128)(2,1)S(1)}, bf16[128,2048]{1,0:T(8,128)(2,1)S(1)}, u32[]{:S(2)}, u32[]{:S(2)}) collective-permute-start(bf16[128,2048]{1,0:T(8,128)(2,1)S(1)} %fusion.112), channel_id=1, source_target_pairs={{1,0},{2,1},{3,2},{4,3},{5,4},{6,5},{7,6},{8,7},{9,8},{10,9},{11,1... | collective-permute-start | bytes 1572872 | tf_op jit(solution)/shard_map/ppermute | solution.py:16
  112.7 6.4 %copy-start.6 = (bf16[1,3,3,2048]{3,2,1,0:T(4,128)(2,1)S(1)}, bf16[1,3,3,2048]{3,2,1,0:T(4,128)(2,1)}, u32[]{:S(2)}) copy-start(bf16[1,3,3,2048]{3,2,1,0:T(4,128)(2,1)} %param.12) | copy-start | bytes 110596
  112.7 6.6 %copy-start.3 = (bf16[128,2048]{1,0:T(8,128)(2,1)S(1)}, bf16[128,2048]{1,0:T(8,128)(2,1)}, u32[]{:S(2)}) copy-start(bf16[128,2048]{1,0:T(8,128)(2,1)} %copy-done.2) | copy-start | bytes 1572868
  115.3 11.7 %collective-permute-start.1 = (bf16[128,2048]{1,0:T(8,128)(2,1)S(1)}, bf16[128,2048]{1,0:T(8,128)(2,1)}, u32[]{:S(2)}, u32[]{:S(2)}) collective-permute-start(bf16[128,2048]{1,0:T(8,128)(2,1)S(1)} %get-tuple-element.492), channel_id=1, source_target_pairs={{0,1},{1,2},{2,3},{3,4},{4,5},{5,6},{6,7},{7,8},{8,9},{9,10},{10,1... | collective-permute-start | bytes 1572872 | tf_op jit(solution)/shard_map/ppermute | solution.py:16
  309.2 1.5 copy-start
  309.2 1.5 copy-start.1
  311.0 3.4 collective-permute-start.3
Sparse Core Ops, SparseCore 0:
  313.2 89.0 all-reduce.1
where the time goes:
time: 411 us
  other arithmetic  200 us (49%)
  waiting for transfers between devices  111 us (27%)
  local copies, waits for them, and re-layouts  61.2 us (15%)
  between operations  14.3 us (3%)
  loops' own time  14.2 us (3%)
  starting transfers between devices  9.31 us (2%)
    psum x1, waiting for transfers between devices, body(): summed = lax.psum(filter_sum, 'ctx')  85.1 us
    add x8, other arithmetic, forward_step(): total = total + jnp.where(usable, shifted * weights[None, :], 0.0)  76.8 us
    reduce_sum x8, other arithmetic, forward_step(): jnp.sum((grad_wide * shifted).reshape(row_count, groups, members), axis=2)  55.5 us
    add x8, other arithmetic, step(): total + jnp.where((lag <= ahead_pos)[:, None], ahead * weights[None, :],...  44.8 us
    ppermute x3, waiting for transfers between devices, shifted_2(): return lax.ppermute(block, axis, route)  13.8 us
    ppermute x1, waiting for transfers between devices, from_behind(): lax.ppermute(shard, axis, [(i, (i + by) % count) for i in range(count)])  12.4 us
    mul x128, local copies, waits for them, and re-layouts, step(): ahead * weights[None, :]  12.2 us
    mul x128, local copies, waits for them, and re-layouts, forward_step(): total = total + jnp.where(usable, shifted * weights[None, :], 0.0)  12.2 us
  transfers between devices with their start and end apart: 5, of which 5 were waited for; matrix products, arithmetic and copies ran while one was open for 1% of the time, Pallas kernels for 0%

commit v1 on v0

--- a/solution.py
+++ b/solution.py
@@ -1,8 +1,21 @@
+import functools
 import math
 import jax
 import jax.numpy as jnp
 from jax import lax
 from jax.sharding import PartitionSpec as P
+
+
+def carry_patch(x_part, comm_axis):
+    n_slots = lax.psum(1, comm_axis)
+    fresh = x_part
+    base_arr = lambda spare: [(idx, idx ^ spare) for idx in range(n_slots)]
+    for no in range(n_slots.bit_length() - 1):
+        fresh = fresh + lax.ppermute(fresh, comm_axis, base_arr(1 << no))
+    return fresh
+
+
+run_clusters_by_axis = functools.partial(carry_patch, comm_axis="ctx")
 
 
 def from_behind(shard, axis, by):
@@ -100,7 +113,7 @@
             0.0,
         )
     grad_pre = total.astype(jnp.bfloat16)[None]
-    summed = lax.psum(filter_sum, "ctx")
+    summed = run_clusters_by_axis(filter_sum)
     filter_grad = (summed / math.sqrt(row_count * devices * members))[None]
     return (grad_pre, filter_grad)
 

time: 411 us -> 324 us (0.79)
  waiting for transfers between devices: 111 us -> 31.5 us
  between operations: 14.3 us -> 0.95 us
  starting transfers between devices: 9.31 us -> 14.2 us
    psum x1 -> x0, waiting for transfers between devices: 85.1 us -> none  [body(): summed = lax.psum(filter_sum, 'ctx')]
    ppermute x0 -> x4, waiting for transfers between devices: none -> 6.72 us  [carry_patch(): fresh = fresh + lax.ppermute(fresh, comm_axis, base_arr(1 << no))]
    ppermute x0 -> x4, starting transfers between devices: none -> 4.34 us  [carry_patch(): fresh = fresh + lax.ppermute(fresh, comm_axis, base_arr(1 << no))]
  transfers between devices with their start and end apart: 5 -> 8, of which waited for: 5 -> 5; matrix products, arithmetic and copies ran while one was open for 1% -> 2% of each run, Pallas kernels for 0% -> 0%
where the time goes in v1:
time: 324 us; the launch traced here: 322 us
  other arithmetic  200 us (62%)
  local copies, waits for them, and re-layouts  61.2 us (19%)
  waiting for transfers between devices  31.5 us (10%)
  loops' own time  14.3 us (4%)
  starting transfers between devices  14.2 us (4%)
    add x8, other arithmetic, forward_step(): total = total + jnp.where(usable, shifted * weights[None, :], 0.0)  76.4 us
    reduce_sum x8, other arithmetic, forward_step(): jnp.sum((grad_wide * shifted).reshape(row_count, groups, members), axis=2)  55 us
    add x8, other arithmetic, step(): total + jnp.where((lag <= ahead_pos)[:, None], ahead * weights[None, :],...  44.8 us
    ppermute x3, waiting for transfers between devices, shifted_2(): return lax.ppermute(block, axis, route)  12.5 us
    ppermute x1, waiting for transfers between devices, from_behind(): lax.ppermute(shard, axis, [(i, (i + by) % count) for i in range(count)])  12.4 us
    mul x128, local copies, waits for them, and re-layouts, step(): ahead * weights[None, :]  12.2 us
    mul x128, local copies, waits for them, and re-layouts, forward_step(): total = total + jnp.where(usable, shifted * weights[None, :], 0.0)  12.2 us
    dynamic_slice x16, local copies, waits for them, and re-layouts, body(): lax.scan(forward_step, jnp.zeros((row_count, channels), jnp.float32), bases)  10 us
  transfers between devices with their start and end apart: 8, of which 5 were waited for; matrix products, arithmetic and copies ran while one was open for 2% of the time, Pallas kernels for 0%

profile of v1, /device:TPU:8, one launch (start us, length us, event | category | flops | bytes accessed | tf_op | source)
XLA Modules:
  0.0 321.6 jit_solution(1417006654464104880)
XLA Ops:
  0.6 1.6 collective-permute-start
  2.2 12.4 %collective-permute-done = bf16[128,2048]{1,0:T(8,128)(2,1)S(1)} collective-permute-done((bf16[128,2048]{1,0:T(8,128)(2,1)}, bf16[128,2048]{1,0:T(8,128)(2,1)S(1)}, u32[]{:S(2)}, u32[]{:S(2)}) %collective-permute-start) | collective-permute-done | bytes 524320 | tf_op jit(solution)/shard_map/ppermute | solution.py:23
  14.6 1.4 fusion.112
  16.0 1.9 collective-permute-start.2
  18.0 0.7 copy.16
  18.9 0.7 sub.118
  19.6 5.0 %collective-permute-done.2 = bf16[128,2048]{1,0:T(8,128)(2,1)S(1)} collective-permute-done((bf16[128,2048]{1,0:T(8,128)(2,1)S(1)}, bf16[128,2048]{1,0:T(8,128)(2,1)S(1)}, u32[]{:S(2)}, u32[]{:S(2)}) %collective-permute-start.2) | collective-permute-done | bytes 524320 | tf_op jit(solution)/shard_map/ppermute | solution.py:29
  24.8 81.4 %while.30 = (s32[]{:T(128)}, f32[128,2048]{1,0:T(8,128)S(1)}, s32[8]{0:T(128)S(1)}, s32[256]{0:T(256)S(1)}, bf16[256,2048]{1,0:T(8,128)(2,1)S(1)}, /*index=5*/bf...) while((s32[]{:T(128)}, f32[128,2048]{1,0:T(8,128)S(1)}, ...), condition=%wide.region_37.38_spmd.clone, body=%wide.region_36.37_spmd.clone.sunk | while | flops 17043556 | bytes 11044691 | solution.py:46
  24.8 0.7 dynamic_slice.941
  29.3 5.6 %fusion.128 = f32[128,2048]{1,0:T(8,128)S(1)} fusion(f32[128,2048]{1,0:T(8,128)S(1)} %get-tuple-element.835, f32[2048]{0:T(1024)S(1)} %mul.1435, bf16[256,2048]{1,0:T(8,128)(2,1)S(1)} %get-tuple-element.893, s32[]{:T(128)S(6)} %select_n.1196, f32[2048]{0:T(1024)S(1)} %mul.1436, s32[]{:T(128)S(6)} %select_n.1197, f32[2048]{0:T(1024)S(1)} %mul.1437, ...), kind=kLoop, calls=%fused_computation.176.clone.1 | loop fusion | flops 17039360 | bytes 10618945 | tf_op jit(solution)/shard_map/while/body/eval_jaxpr/add | solution.py:42
  34.9 0.7 dynamic_slice.941
  39.5 5.6 %fusion.128 = f32[128,2048]{1,0:T(8,128)S(1)} fusion(f32[128,2048]{1,0:T(8,128)S(1)} %get-tuple-element.835, f32[2048]{0:T(1024)S(1)} %mul.1435, bf16[256,2048]{1,0:T(8,128)(2,1)S(1)} %get-tuple-element.893, s32[]{:T(128)S(6)} %select_n.1196, f32[2048]{0:T(1024)S(1)} %mul.1436, s32[]{:T(128)S(6)} %select_n.1197, f32[2048]{0:T(1024)S(1)} %mul.1437, ...), kind=kLoop, calls=%fused_computation.176.clone.1 | loop fusion | flops 17039360 | bytes 10618945 | tf_op jit(solution)/shard_map/while/body/eval_jaxpr/add | solution.py:42
  45.1 0.7 dynamic_slice.941
  49.7 5.6 %fusion.128 = f32[128,2048]{1,0:T(8,128)S(1)} fusion(f32[128,2048]{1,0:T(8,128)S(1)} %get-tuple-element.835, f32[2048]{0:T(1024)S(1)} %mul.1435, bf16[256,2048]{1,0:T(8,128)(2,1)S(1)} %get-tuple-element.893, s32[]{:T(128)S(6)} %select_n.1196, f32[2048]{0:T(1024)S(1)} %mul.1436, s32[]{:T(128)S(6)} %select_n.1197, f32[2048]{0:T(1024)S(1)} %mul.1437, ...), kind=kLoop, calls=%fused_computation.176.clone.1 | loop fusion | flops 17039360 | bytes 10618945 | tf_op jit(solution)/shard_map/while/body/eval_jaxpr/add | solution.py:42
  55.3 0.7 dynamic_slice.941
  59.8 5.6 %fusion.128 = f32[128,2048]{1,0:T(8,128)S(1)} fusion(f32[128,2048]{1,0:T(8,128)S(1)} %get-tuple-element.835, f32[2048]{0:T(1024)S(1)} %mul.1435, bf16[256,2048]{1,0:T(8,128)(2,1)S(1)} %get-tuple-element.893, s32[]{:T(128)S(6)} %select_n.1196, f32[2048]{0:T(1024)S(1)} %mul.1436, s32[]{:T(128)S(6)} %select_n.1197, f32[2048]{0:T(1024)S(1)} %mul.1437, ...), kind=kLoop, calls=%fused_computation.176.clone.1 | loop fusion | flops 17039360 | bytes 10618945 | tf_op jit(solution)/shard_map/while/body/eval_jaxpr/add | solution.py:42
  65.5 0.7 dynamic_slice.941
  70.0 5.6 %fusion.128 = f32[128,2048]{1,0:T(8,128)S(1)} fusion(f32[128,2048]{1,0:T(8,128)S(1)} %get-tuple-element.835, f32[2048]{0:T(1024)S(1)} %mul.1435, bf16[256,2048]{1,0:T(8,128)(2,1)S(1)} %get-tuple-element.893, s32[]{:T(128)S(6)} %select_n.1196, f32[2048]{0:T(1024)S(1)} %mul.1436, s32[]{:T(128)S(6)} %select_n.1197, f32[2048]{0:T(1024)S(1)} %mul.1437, ...), kind=kLoop, calls=%fused_computation.176.clone.1 | loop fusion | flops 17039360 | bytes 10618945 | tf_op jit(solution)/shard_map/while/body/eval_jaxpr/add | solution.py:42
  75.6 0.7 dynamic_slice.941
  80.2 5.6 %fusion.128 = f32[128,2048]{1,0:T(8,128)S(1)} fusion(f32[128,2048]{1,0:T(8,128)S(1)} %get-tuple-element.835, f32[2048]{0:T(1024)S(1)} %mul.1435, bf16[256,2048]{1,0:T(8,128)(2,1)S(1)} %get-tuple-element.893, s32[]{:T(128)S(6)} %select_n.1196, f32[2048]{0:T(1024)S(1)} %mul.1436, s32[]{:T(128)S(6)} %select_n.1197, f32[2048]{0:T(1024)S(1)} %mul.1437, ...), kind=kLoop, calls=%fused_computation.176.clone.1 | loop fusion | flops 17039360 | bytes 10618945 | tf_op jit(solution)/shard_map/while/body/eval_jaxpr/add | solution.py:42
  85.8 0.7 dynamic_slice.941
  90.3 5.6 %fusion.128 = f32[128,2048]{1,0:T(8,128)S(1)} fusion(f32[128,2048]{1,0:T(8,128)S(1)} %get-tuple-element.835, f32[2048]{0:T(1024)S(1)} %mul.1435, bf16[256,2048]{1,0:T(8,128)(2,1)S(1)} %get-tuple-element.893, s32[]{:T(128)S(6)} %select_n.1196, f32[2048]{0:T(1024)S(1)} %mul.1436, s32[]{:T(128)S(6)} %select_n.1197, f32[2048]{0:T(1024)S(1)} %mul.1437, ...), kind=kLoop, calls=%fused_computation.176.clone.1 | loop fusion | flops 17039360 | bytes 10618945 | tf_op jit(solution)/shard_map/while/body/eval_jaxpr/add | solution.py:42
  96.0 0.7 dynamic_slice.941
  100.5 5.6 %fusion.128 = f32[128,2048]{1,0:T(8,128)S(1)} fusion(f32[128,2048]{1,0:T(8,128)S(1)} %get-tuple-element.835, f32[2048]{0:T(1024)S(1)} %mul.1435, bf16[256,2048]{1,0:T(8,128)(2,1)S(1)} %get-tuple-element.893, s32[]{:T(128)S(6)} %select_n.1196, f32[2048]{0:T(1024)S(1)} %mul.1436, s32[]{:T(128)S(6)} %select_n.1197, f32[2048]{0:T(1024)S(1)} %mul.1437, ...), kind=kLoop, calls=%fused_computation.176.clone.1 | loop fusion | flops 17039360 | bytes 10618945 | tf_op jit(solution)/shard_map/while/body/eval_jaxpr/add | solution.py:42
  106.2 2.6 fusion.118
  108.8 3.8 %collective-permute-start.1 = (bf16[128,2048]{1,0:T(8,128)(2,1)S(1)}, bf16[128,2048]{1,0:T(8,128)(2,1)}, u32[]{:S(2)}, u32[]{:S(2)}) collective-permute-start(bf16[128,2048]{1,0:T(8,128)(2,1)S(1)} %get-tuple-element.492), channel_id=1, source_target_pairs={{0,1},{1,2},{2,3},{3,4},{4,5},{5,6},{6,7},{7,8},{8,9},{9,10},{10,1... | collective-permute-start | bytes 1572872 | tf_op jit(solution)/shard_map/ppermute | solution.py:29
  113.0 7.5 %collective-permute-done.1 = bf16[128,2048]{1,0:T(8,128)(2,1)} collective-permute-done((bf16[128,2048]{1,0:T(8,128)(2,1)S(1)}, bf16[128,2048]{1,0:T(8,128)(2,1)}, u32[]{:S(2)}, u32[]{:S(2)}) %collective-permute-start.1) | collective-permute-done | bytes 524320 | tf_op jit(solution)/shard_map/ppermute | solution.py:29
  120.4 2.2 pad_maximum_fusion.2
  122.6 1.5 copy.17
  124.1 177.8 %while.29 = (s32[]{:T(128)}, f32[128,2048]{0,1:T(8,128)S(1)}, f32[8,16,128]{2,1,0:T(8,128)}, s32[8]{0:T(128)S(1)}, s32[128]{0:T(128)S(1)}, /*index=5*/bf16[256,2...) while((s32[]{:T(128)}, f32[128,2048]{0,1:T(8,128)S(1)}, ...), condition=%wide.region_35.36_spmd.clone, body=%wide.region_2.35_spmd.clone.sunk | while | flops 30148740 | bytes 21566524 | solution.py:92
  124.1 0.6 dynamic_slice.921
  125.5 6.9 %bitcast_reduce_fusion.17 = (bf16[128,128]{0,1:T(8,128)(2,1)S(1)}, bf16[128,128]{0,1:T(8,128)(2,1)S(1)}, bf16[128,128]{0,1:T(8,128)(2,1)S(1)}, bf16[128,128]{0,1...) fusion(f32[128,2048]{0,1:T(8,128)S(1)} %get-tuple-element.1035,, ...), kind=kLoop, calls=%fused_computation.64.clone.1 | loop fusion | flops 12320768 | bytes 9961536 | tf_op jit(solution)/shard_map/while/body/eval_jaxpr/reduce_sum | solution.py:84
  133.4 0.6 constant_dynamic-update-slice_fusion.2
  136.8 9.6 %fusion.126 = f32[128,2048]{0,1:T(8,128)S(1)} fusion(f32[128,2048]{0,1:T(8,128)S(1)} %get-tuple-element.987, f32[2048]{0:T(1024)S(1)} %mul.1386, f32[2048]{0:T(1024)S(1)} %mul.1387, f32[2048]{0:T(1024)S(1)} %mul.1388, f32[2048]{0:T(1024)S(1)} %mul.1389, f32[2048]{0:T(1024)S(1)} %mul.1390, f32[2048]{0:T(1024)S(1)} %mul.1391, f32[2048]{0:T(1024)S(1)} %mul.1392, ...), kind=kLoop, calls=%fused_computation.48.clone.1 | loop fusion | flops 17039360 | bytes 10618945 | tf_op jit(solution)/shard_map/while/body/eval_jaxpr/add | solution.py:83
  147.7 6.9 %bitcast_reduce_fusion.17 = (bf16[128,128]{0,1:T(8,128)(2,1)S(1)}, bf16[128,128]{0,1:T(8,128)(2,1)S(1)}, bf16[128,128]{0,1:T(8,128)(2,1)S(1)}, bf16[128,128]{0,1...) fusion(f32[128,2048]{0,1:T(8,128)S(1)} %get-tuple-element.1035,, ...), kind=kLoop, calls=%fused_computation.64.clone.1 | loop fusion | flops 12320768 | bytes 9961536 | tf_op jit(solution)/shard_map/while/body/eval_jaxpr/reduce_sum | solution.py:84
  155.7 0.6 constant_dynamic-update-slice_fusion.2
  159.0 9.6 %fusion.126 = f32[128,2048]{0,1:T(8,128)S(1)} fusion(f32[128,2048]{0,1:T(8,128)S(1)} %get-tuple-element.987, f32[2048]{0:T(1024)S(1)} %mul.1386, f32[2048]{0:T(1024)S(1)} %mul.1387, f32[2048]{0:T(1024)S(1)} %mul.1388, f32[2048]{0:T(1024)S(1)} %mul.1389, f32[2048]{0:T(1024)S(1)} %mul.1390, f32[2048]{0:T(1024)S(1)} %mul.1391, f32[2048]{0:T(1024)S(1)} %mul.1392, ...), kind=kLoop, calls=%fused_computation.48.clone.1 | loop fusion | flops 17039360 | bytes 10618945 | tf_op jit(solution)/shard_map/while/body/eval_jaxpr/add | solution.py:83
  170.0 6.9 %bitcast_reduce_fusion.17 = (bf16[128,128]{0,1:T(8,128)(2,1)S(1)}, bf16[128,128]{0,1:T(8,128)(2,1)S(1)}, bf16[128,128]{0,1:T(8,128)(2,1)S(1)}, bf16[128,128]{0,1...) fusion(f32[128,2048]{0,1:T(8,128)S(1)} %get-tuple-element.1035,, ...), kind=kLoop, calls=%fused_computation.64.clone.1 | loop fusion | flops 12320768 | bytes 9961536 | tf_op jit(solution)/shard_map/while/body/eval_jaxpr/reduce_sum | solution.py:84
  177.9 0.6 constant_dynamic-update-slice_fusion.2
  181.2 9.6 %fusion.126 = f32[128,2048]{0,1:T(8,128)S(1)} fusion(f32[128,2048]{0,1:T(8,128)S(1)} %get-tuple-element.987, f32[2048]{0:T(1024)S(1)} %mul.1386, f32[2048]{0:T(1024)S(1)} %mul.1387, f32[2048]{0:T(1024)S(1)} %mul.1388, f32[2048]{0:T(1024)S(1)} %mul.1389, f32[2048]{0:T(1024)S(1)} %mul.1390, f32[2048]{0:T(1024)S(1)} %mul.1391, f32[2048]{0:T(1024)S(1)} %mul.1392, ...), kind=kLoop, calls=%fused_computation.48.clone.1 | loop fusion | flops 17039360 | bytes 10618945 | tf_op jit(solution)/shard_map/while/body/eval_jaxpr/add | solution.py:83
  192.2 6.9 %bitcast_reduce_fusion.17 = (bf16[128,128]{0,1:T(8,128)(2,1)S(1)}, bf16[128,128]{0,1:T(8,128)(2,1)S(1)}, bf16[128,128]{0,1:T(8,128)(2,1)S(1)}, bf16[128,128]{0,1...) fusion(f32[128,2048]{0,1:T(8,128)S(1)} %get-tuple-element.1035,, ...), kind=kLoop, calls=%fused_computation.64.clone.1 | loop fusion | flops 12320768 | bytes 9961536 | tf_op jit(solution)/shard_map/while/body/eval_jaxpr/reduce_sum | solution.py:84
  200.1 0.6 constant_dynamic-update-slice_fusion.2
  203.5 9.6 %fusion.126 = f32[128,2048]{0,1:T(8,128)S(1)} fusion(f32[128,2048]{0,1:T(8,128)S(1)} %get-tuple-element.987, f32[2048]{0:T(1024)S(1)} %mul.1386, f32[2048]{0:T(1024)S(1)} %mul.1387, f32[2048]{0:T(1024)S(1)} %mul.1388, f32[2048]{0:T(1024)S(1)} %mul.1389, f32[2048]{0:T(1024)S(1)} %mul.1390, f32[2048]{0:T(1024)S(1)} %mul.1391, f32[2048]{0:T(1024)S(1)} %mul.1392, ...), kind=kLoop, calls=%fused_computation.48.clone.1 | loop fusion | flops 17039360 | bytes 10618945 | tf_op jit(solution)/shard_map/while/body/eval_jaxpr/add | solution.py:83
  214.4 6.9 %bitcast_reduce_fusion.17 = (bf16[128,128]{0,1:T(8,128)(2,1)S(1)}, bf16[128,128]{0,1:T(8,128)(2,1)S(1)}, bf16[128,128]{0,1:T(8,128)(2,1)S(1)}, bf16[128,128]{0,1...) fusion(f32[128,2048]{0,1:T(8,128)S(1)} %get-tuple-element.1035,, ...), kind=kLoop, calls=%fused_computation.64.clone.1 | loop fusion | flops 12320768 | bytes 9961536 | tf_op jit(solution)/shard_map/while/body/eval_jaxpr/reduce_sum | solution.py:84
  222.3 0.6 constant_dynamic-update-slice_fusion.2
  225.7 9.6 %fusion.126 = f32[128,2048]{0,1:T(8,128)S(1)} fusion(f32[128,2048]{0,1:T(8,128)S(1)} %get-tuple-element.987, f32[2048]{0:T(1024)S(1)} %mul.1386, f32[2048]{0:T(1024)S(1)} %mul.1387, f32[2048]{0:T(1024)S(1)} %mul.1388, f32[2048]{0:T(1024)S(1)} %mul.1389, f32[2048]{0:T(1024)S(1)} %mul.1390, f32[2048]{0:T(1024)S(1)} %mul.1391, f32[2048]{0:T(1024)S(1)} %mul.1392, ...), kind=kLoop, calls=%fused_computation.48.clone.1 | loop fusion | flops 17039360 | bytes 10618945 | tf_op jit(solution)/shard_map/while/body/eval_jaxpr/add | solution.py:83
  236.6 6.9 %bitcast_reduce_fusion.17 = (bf16[128,128]{0,1:T(8,128)(2,1)S(1)}, bf16[128,128]{0,1:T(8,128)(2,1)S(1)}, bf16[128,128]{0,1:T(8,128)(2,1)S(1)}, bf16[128,128]{0,1...) fusion(f32[128,2048]{0,1:T(8,128)S(1)} %get-tuple-element.1035,, ...), kind=kLoop, calls=%fused_computation.64.clone.1 | loop fusion | flops 12320768 | bytes 9961536 | tf_op jit(solution)/shard_map/while/body/eval_jaxpr/reduce_sum | solution.py:84
  244.6 0.6 constant_dynamic-update-slice_fusion.2
  247.9 9.6 %fusion.126 = f32[128,2048]{0,1:T(8,128)S(1)} fusion(f32[128,2048]{0,1:T(8,128)S(1)} %get-tuple-element.987, f32[2048]{0:T(1024)S(1)} %mul.1386, f32[2048]{0:T(1024)S(1)} %mul.1387, f32[2048]{0:T(1024)S(1)} %mul.1388, f32[2048]{0:T(1024)S(1)} %mul.1389, f32[2048]{0:T(1024)S(1)} %mul.1390, f32[2048]{0:T(1024)S(1)} %mul.1391, f32[2048]{0:T(1024)S(1)} %mul.1392, ...), kind=kLoop, calls=%fused_computation.48.clone.1 | loop fusion | flops 17039360 | bytes 10618945 | tf_op jit(solution)/shard_map/while/body/eval_jaxpr/add | solution.py:83
  258.9 6.9 %bitcast_reduce_fusion.17 = (bf16[128,128]{0,1:T(8,128)(2,1)S(1)}, bf16[128,128]{0,1:T(8,128)(2,1)S(1)}, bf16[128,128]{0,1:T(8,128)(2,1)S(1)}, bf16[128,128]{0,1...) fusion(f32[128,2048]{0,1:T(8,128)S(1)} %get-tuple-element.1035,, ...), kind=kLoop, calls=%fused_computation.64.clone.1 | loop fusion | flops 12320768 | bytes 9961536 | tf_op jit(solution)/shard_map/while/body/eval_jaxpr/reduce_sum | solution.py:84
  266.8 0.6 constant_dynamic-update-slice_fusion.2
  270.1 9.6 %fusion.126 = f32[128,2048]{0,1:T(8,128)S(1)} fusion(f32[128,2048]{0,1:T(8,128)S(1)} %get-tuple-element.987, f32[2048]{0:T(1024)S(1)} %mul.1386, f32[2048]{0:T(1024)S(1)} %mul.1387, f32[2048]{0:T(1024)S(1)} %mul.1388, f32[2048]{0:T(1024)S(1)} %mul.1389, f32[2048]{0:T(1024)S(1)} %mul.1390, f32[2048]{0:T(1024)S(1)} %mul.1391, f32[2048]{0:T(1024)S(1)} %mul.1392, ...), kind=kLoop, calls=%fused_computation.48.clone.1 | loop fusion | flops 17039360 | bytes 10618945 | tf_op jit(solution)/shard_map/while/body/eval_jaxpr/add | solution.py:83
  281.1 6.9 %bitcast_reduce_fusion.17 = (bf16[128,128]{0,1:T(8,128)(2,1)S(1)}, bf16[128,128]{0,1:T(8,128)(2,1)S(1)}, bf16[128,128]{0,1:T(8,128)(2,1)S(1)}, bf16[128,128]{0,1...) fusion(f32[128,2048]{0,1:T(8,128)S(1)} %get-tuple-element.1035,, ...), kind=kLoop, calls=%fused_computation.64.clone.1 | loop fusion | flops 12320768 | bytes 9961536 | tf_op jit(solution)/shard_map/while/body/eval_jaxpr/reduce_sum | solution.py:84
  289.0 0.6 constant_dynamic-update-slice_fusion.2
  292.4 9.6 %fusion.126 = f32[128,2048]{0,1:T(8,128)S(1)} fusion(f32[128,2048]{0,1:T(8,128)S(1)} %get-tuple-element.987, f32[2048]{0:T(1024)S(1)} %mul.1386, f32[2048]{0:T(1024)S(1)} %mul.1387, f32[2048]{0:T(1024)S(1)} %mul.1388, f32[2048]{0:T(1024)S(1)} %mul.1389, f32[2048]{0:T(1024)S(1)} %mul.1390, f32[2048]{0:T(1024)S(1)} %mul.1391, f32[2048]{0:T(1024)S(1)} %mul.1392, ...), kind=kLoop, calls=%fused_computation.48.clone.1 | loop fusion | flops 17039360 | bytes 10618945 | tf_op jit(solution)/shard_map/while/body/eval_jaxpr/add | solution.py:83
  302.4 1.2 fusion.119
  303.8 2.5 collective-permute-start.3
  306.3 0.9 bitcast_add_fusion
  307.1 1.5 collective-permute-start.5
  308.8 2.6 collective-permute-done.5
  311.6 4.1 %collective-permute-done.6 = f32[128,128]{1,0:T(8,128)S(1)} collective-permute-done((f32[128,128]{1,0:T(8,128)S(1)}, f32[128,128]{1,0:T(8,128)S(1)}, u32[]{:S(2)}, u32[]{:S(2)}) %collective-permute-start.6) | collective-permute-done | bytes 65568 | tf_op jit(solution)/shard_map/ppermute | solution.py:14
  315.7 2.7 collective-permute-start.7
  318.4 2.6 fusion.111
  321.0 0.6 multiply_bitcast_fusion
  (673 shorter events, 59.5 us)
Async XLA Ops:
  0.6 24.1 %copy-start.5 = (bf16[1,128,128]{2,1,0:T(8,128)(2,1)S(1)}, bf16[1,128,128]{2,1,0:T(8,128)(2,1)}, u32[]{:S(2)}) copy-start(bf16[1,128,128]{2,1,0:T(8,128)(2,1)} %param.11) | copy-start | bytes 98308
  0.6 13.9 %collective-permute-start = (bf16[128,2048]{1,0:T(8,128)(2,1)}, bf16[128,2048]{1,0:T(8,128)(2,1)S(1)}, u32[]{:S(2)}, u32[]{:S(2)}) collective-permute-start(bf16[128,2048]{1,0:T(8,128)(2,1)} %bitcast.310), channel_id=1, source_target_pairs={{0,16},{16,0},{1,17},{17,1},{2,18},{18,2},{3,19},{19,3},{4,20},{20... | collective-permute-start | bytes 1572872 | tf_op jit(solution)/shard_map/ppermute | solution.py:23
  14.6 3.4 %copy-start.4 = (bf16[128,2048]{1,0:T(8,128)(2,1)}, bf16[128,2048]{1,0:T(8,128)(2,1)S(1)}, u32[]{:S(2)}) copy-start(bf16[128,2048]{1,0:T(8,128)(2,1)S(1)} %collective-permute-done) | copy-start | bytes 1572868
  16.0 8.7 %copy-start.2 = (bf16[128,2048]{1,0:T(8,128)(2,1)}, bf16[128,2048]{1,0:T(8,128)(2,1)S(1)}, u32[]{:S(2)}) copy-start(bf16[128,2048]{1,0:T(8,128)(2,1)S(1)} %fusion.112) | copy-start | bytes 1572868
  16.0 8.6 %collective-permute-start.2 = (bf16[128,2048]{1,0:T(8,128)(2,1)S(1)}, bf16[128,2048]{1,0:T(8,128)(2,1)S(1)}, u32[]{:S(2)}, u32[]{:S(2)}) collective-permute-start(bf16[128,2048]{1,0:T(8,128)(2,1)S(1)} %fusion.112), channel_id=1, source_target_pairs={{1,0},{2,1},{3,2},{4,3},{5,4},{6,5},{7,6},{8,7},{9,8},{10,9},{11,1... | collective-permute-start | bytes 1572872 | tf_op jit(solution)/shard_map/ppermute | solution.py:29
  106.1 6.5 %copy-start.6 = (bf16[1,3,3,2048]{3,2,1,0:T(4,128)(2,1)S(1)}, bf16[1,3,3,2048]{3,2,1,0:T(4,128)(2,1)}, u32[]{:S(2)}) copy-start(bf16[1,3,3,2048]{3,2,1,0:T(4,128)(2,1)} %param.12) | copy-start | bytes 110596
  106.2 6.6 %copy-start.3 = (bf16[128,2048]{1,0:T(8,128)(2,1)S(1)}, bf16[128,2048]{1,0:T(8,128)(2,1)}, u32[]{:S(2)}) copy-start(bf16[128,2048]{1,0:T(8,128)(2,1)} %copy-done.2) | copy-start | bytes 1572868
  108.8 11.7 %collective-permute-start.1 = (bf16[128,2048]{1,0:T(8,128)(2,1)S(1)}, bf16[128,2048]{1,0:T(8,128)(2,1)}, u32[]{:S(2)}, u32[]{:S(2)}) collective-permute-start(bf16[128,2048]{1,0:T(8,128)(2,1)S(1)} %get-tuple-element.492), channel_id=1, source_target_pairs={{0,1},{1,2},{2,3},{3,4},{4,5},{5,6},{6,7},{7,8},{8,9},{9,10},{10,1... | collective-permute-start | bytes 1572872 | tf_op jit(solution)/shard_map/ppermute | solution.py:29
  301.9 4.3 %collective-permute-start.4 = (f32[128,128]{1,0:T(8,128)}, f32[128,128]{1,0:T(8,128)S(1)}, u32[]{:S(2)}, u32[]{:S(2)}) collective-permute-start(f32[128,128]{1,0:T(8,128)} %bitcast.13), channel_id=1, source_target_pairs={{0,1},{1,0},{2,3},{3,2},{4,5},{5,4},{6,7},{7,6},{8,9},{9,8},{10,11... | collective-permute-start | bytes 196616 | tf_op jit(solution)/shard_map/ppermute | solution.py:14
  302.0 1.5 copy-start
  302.0 1.5 copy-start.1
  303.8 7.7 %collective-permute-start.3 = (bf16[3,2,2048]{2,1,0:T(2,128)(2,1)S(1)}, bf16[3,2,2048]{2,1,0:T(2,128)(2,1)S(1)}, u32[]{:S(2)}, u32[]{:S(2)}) collective-permute-start(bf16[3,2,2048]{2,1,0:T(2,128)(2,1)S(1)} %slice.51), channel_id=1, source_target_pairs={{1,0},{2,1},{3,2},{4,3},{5,4},{6,5},{7,6},{8,7},{9,8},{10,9},{11,1... | collective-permute-start | bytes 73736 | tf_op jit(solution)/shard_map/ppermute | solution.py:29
  307.1 4.3 %collective-permute-start.5 = (f32[128,128]{1,0:T(8,128)S(1)}, f32[128,128]{1,0:T(8,128)S(1)}, u32[]{:S(2)}, u32[]{:S(2)}) collective-permute-start(f32[128,128]{1,0:T(8,128)S(1)} %bitcast_add_fusion), channel_id=1, source_target_pairs={{0,2},{1,3},{2,0},{3,1},{4,6},{5,7},{6,4},{7,5},{8,10},{9,11},{10,... | collective-permute-start | bytes 196616 | tf_op jit(solution)/shard_map/ppermute | solution.py:14
  311.4 4.3 %collective-permute-start.6 = (f32[128,128]{1,0:T(8,128)S(1)}, f32[128,128]{1,0:T(8,128)S(1)}, u32[]{:S(2)}, u32[]{:S(2)}) collective-permute-start(f32[128,128]{1,0:T(8,128)S(1)} %add.1045), channel_id=1, source_target_pairs={{0,4},{1,5},{2,6},{3,7},{4,0},{5,1},{6,2},{7,3},{8,12},{9,13},{10,... | collective-permute-start | bytes 196616 | tf_op jit(solution)/shard_map/ppermute | solution.py:14
  315.7 5.2 %collective-permute-start.7 = (f32[128,128]{1,0:T(8,128)S(1)}, f32[128,128]{1,0:T(8,128)S(1)}, u32[]{:S(2)}, u32[]{:S(2)}) collective-permute-start(f32[128,128]{1,0:T(8,128)S(1)} %add.1046), channel_id=1, source_target_pairs={{0,8},{1,9},{2,10},{3,11},{4,12},{5,13},{6,14},{7,15},{8,0},{9,1},... | collective-permute-start | bytes 196616 | tf_op jit(solution)/shard_map/ppermute | solution.py:14
